TPU v7x, 128 devices: a whole 4x4x4 slice. The times are simulated.
128 devices in a mesh: gx: 8 (over z_lo, x), gy: 4 (over z_hi, core), gz: 4 (over y).
Axes of the slice: x: 4, y: 4, z: 4 (z_hi: 2, z_lo: 2; z = z_hi * 2 + z_lo), core: 2. Of those that a mesh axis runs over, the one named last changes fastest.
Arguments:
- x_saved: bfloat16 [1024, 16384], P('gx', ('gy', 'gz')), may hold values from -0.1875 to 0.1875
- grad_out: bfloat16 [1024, 28672], P('gx', ('gz', 'gy')), may hold values from -6 to 6
- weight: bfloat16 [16384, 28672], P('gy', ('gz', 'gx')), may hold values from -0.09375 to 0.09375
Outputs:
- grad_in: bfloat16 [1024, 16384], P('gx', ('gy', 'gz'))
- grad_weight: bfloat16 [16384, 28672], P('gy', ('gz', 'gx'))
All inputs are finite; a program needn't handle non-finite values.
Results may differ from a plain program's by a relative error of at most 0.001.
Values may be sent and summed in bfloat16 or wider, within the bound.
A program may use at most 128 MiB of HBM per device.

v0:
```python
import jax
import jax.numpy as jnp
from jax import lax
from jax.sharding import PartitionSpec as P


def body(x_saved, grad_out, weight):
    token_rows = x_saved.shape[0]
    token_groups = lax.axis_size("gx")
    feature_groups = lax.axis_size("gz")
    grad_block = lax.all_gather(grad_out, "gy", axis=1, tiled=True)
    grad_all = lax.all_to_all(grad_block, "gx", split_axis=1, concat_axis=0, tiled=True)
    unit_cols = grad_all.shape[1]
    inputs_block = lax.all_gather(x_saved, "gz", axis=1, tiled=True)
    summed = jnp.einsum(
        "td,tc->dc",
        lax.all_gather(inputs_block, "gx", axis=0, tiled=True),
        grad_all,
        preferred_element_type=jnp.float32,
    )
    grad_weight = summed.astype(jnp.bfloat16)
    grad_split = grad_all.reshape(token_groups, token_rows, unit_cols)
    weight_split = weight.reshape(feature_groups, weight.shape[0] // feature_groups, unit_cols)
    terms = jnp.einsum(
        "atc,bkc->abtk", grad_split, weight_split, preferred_element_type=jnp.float32
    )
    terms = terms.reshape(token_groups * feature_groups * token_rows, weight_split.shape[1])
    grad_in = lax.psum_scatter(terms, ("gx", "gz"), scatter_dimension=0, tiled=True)
    return (grad_in.astype(jnp.bfloat16), grad_weight)


def solution(mesh):
    return jax.shard_map(
        body,
        mesh=mesh,
        in_specs=(P("gx", ("gy", "gz")), P("gx", ("gz", "gy")), P("gy", ("gz", "gx"))),
        out_specs=(P("gx", ("gy", "gz")), P("gy", ("gz", "gx"))),
        check_vma=False,
    )
```

profile of v0, /device:TPU:0, one launch (start us, length us, event | category | flops | bytes accessed | tf_op | source)
XLA Modules:
  0.0 386.5 jit_solution(9099532467425328987)
XLA Ops:
  7.2 0.0 all-gather.6.cloned.1.call-start
  7.2 0.7 all-gather.6.cloned.1.call-update
  7.9 0.0 all-gather.4.cloned.1.call-start
  7.9 2.0 copy.5
  9.9 0.0 all-gather.4.cloned.1.call-update
  10.0 0.0 all-gather.8.cloned.1.call-start
  10.0 26.1 %all-gather.6.cloned.1.call-done = bf16[128,4096]{1,0:T(8,128)(2,1)} async-done(((bf16[128,1024]{1,0:T(8,128)(2,1)}), bf16[128,4096]{1,0:T(8,128)(2,1)}) %all-gather.6.cloned.1.call-update) | async-done | bytes 1048592 | tf_op jit(solution)/shard_map/all_gather | solution.py:14
  36.1 0.0 all-gather.8.cloned.1.call-update
  36.2 0.0 reduce-scatter.2.cloned.1.call-start
  36.2 27.8 %all-gather.4.cloned.1.call-done = bf16[128,7168]{0,1:T(8,128)(2,1)} async-done(((bf16[128,1792]{0,1:T(8,128)(2,1)}), bf16[128,7168]{0,1:T(8,128)(2,1)}) %all-gather.4.cloned.1.call-update) | async-done | bytes 1835024 | tf_op jit(solution)/shard_map/all_gather | solution.py:11
  64.0 3.1 copy.6
  67.1 46.1 %all_to_all.19 = bf16[128,8,896]{2,0,1:T(8,128)(2,1)S(1)} all-to-all(bf16[128,8,896]{2,0,1:T(8,128)(2,1)S(1)} %copy.6), channel_id=1, replica_groups=mesh['gx'=8,'gy'=4,'gz'=4] {'gx'}, dimensions={1} | all-to-all | bytes 3670016 | tf_op jit(solution)/shard_map/all_to_all | solution.py:12
  113.2 0.0 copy-start
  113.2 11.8 %convolution_bitcast_fusion = f32[8,4,128,1024]{3,2,0,1:T(8,128)S(1)} fusion(bf16[4,1024,896,1]{2,1,3,0:T(8,128)(2,1)} %bitcast.22, bf16[128,8,896]{2,0,1:T(8,128)(2,1)S(1)} %all_to_all.19), kind=kOutput, calls=%fused_computation | convolution fusion | flops 7516192768 | bytes 25952256 | tf_op jit(solution)/shard_map/atc,bkc->abtk/dot_general | solution.py:24
  125.0 0.0 copy-done
  125.0 6.1 %copy.7 = f32[8,4,128,1024]{3,2,1,0:T(8,128)} copy(f32[8,4,128,1024]{3,2,0,1:T(8,128)S(1)} %convolution_bitcast_fusion) | data formatting | bytes 33554432 | tf_op jit(solution)/shard_map/atc,bkc->abtk/transpose | solution.py:24
  131.1 0.0 copy-start.1
  131.1 0.0 reduce-scatter.2.cloned.1.call-update
  131.1 43.9 %all-gather.8.cloned.1.call-done = bf16[1024,4096]{1,0:T(8,128)(2,1)} async-done(((bf16[128,4096]{1,0:T(8,128)(2,1)}), bf16[1024,4096]{1,0:T(8,128)(2,1)}) %all-gather.8.cloned.1.call-update) | async-done | bytes 8388624 | tf_op jit(solution)/shard_map/all_gather | solution.py:17
  175.0 0.0 copy-done.1
  175.1 14.2 %convolution_convert_fusion = bf16[4096,896]{1,0:T(8,128)(2,1)} fusion(bf16[1024,4096]{1,0:T(8,128)(2,1)} %all-gather.8.cloned.1.call-done, bf16[1024,896]{1,0:T(8,128)(2,1)S(1)} %bitcast.21), kind=kOutput, calls=%fused_computation.1 | convolution fusion | flops 7519862784 | bytes 17563648 | tf_op jit(solution)/shard_map/td,tc->dc/dot_general | solution.py:15
  189.3 189.0 %reduce-scatter.2.cloned.1.call-done = f32[128,1024]{1,0:T(8,128)} async-done(((f32[4096,1024]{1,0:T(8,128)}), f32[128,1024]{1,0:T(8,128)}) %reduce-scatter.2.cloned.1.call-update) | async-done | bytes 524304 | tf_op jit(solution)/shard_map/reduce_scatter | solution.py:28
  378.2 1.8 convert_element_type.6
Async XLA Ops:
  7.2 29.0 %all-gather.6.cloned.1.call-start = ((), (), s32[]{:S(2)}) async-start(), calls=%async_computation.4 | async-start | bytes 1310720 | tf_op jit(solution)/shard_map/all_gather | solution.py:14
  7.9 56.1 %all-gather.4.cloned.1.call-start = ((), (), s32[]{:S(2)}) async-start(), calls=%async_computation.2 | async-start | bytes 2293760 | tf_op jit(solution)/shard_map/all_gather | solution.py:11
  10.0 165.1 %all-gather.8.cloned.1.call-start = ((), (), s32[]{:S(2)}) async-start(), calls=%async_computation.5 | async-start | bytes 9437184 | tf_op jit(solution)/shard_map/all_gather | solution.py:17
  36.2 342.1 %reduce-scatter.2.cloned.1.call-start = ((), (), s32[]{:S(2)}) async-start(), calls=%async_computation.3 | async-start | bytes 17301504 | tf_op jit(solution)/shard_map/reduce_scatter | solution.py:28
  113.2 11.8 %copy-start = (bf16[128,8,896]{2,0,1:T(8,128)(2,1)}, bf16[128,8,896]{2,0,1:T(8,128)(2,1)S(1)}, u32[]{:S(2)}) copy-start(bf16[128,8,896]{2,0,1:T(8,128)(2,1)S(1)} %all_to_all.19) | copy-start | bytes 5505028
  131.1 43.9 %copy-start.1 = (bf16[128,8,896]{2,0,1:T(8,128)(2,1)S(1)}, bf16[128,8,896]{2,0,1:T(8,128)(2,1)}, u32[]{:S(2)}) copy-start(bf16[128,8,896]{2,0,1:T(8,128)(2,1)} %copy-done) | copy-start | bytes 5505028
Sparse Core Ops, SparseCore 0:
  9.7 26.4 all-gather.5
  38.4 25.6 all-gather.3
  65.7 109.3 all-gather.7
  177.3 200.8 reduce-scatter.1
where the time goes:
time: 387 us
  waiting for transfers between devices  288 us (74%)
  blocking collectives  46.1 us (12%)
  matrix products  26 us (7%)
  between operations  13.8 us (4%)
  local copies, waits for them, and re-layouts  11.2 us (3%)
    reduce_scatter x1, waiting for transfers between devices, body(): lax.psum_scatter(terms, ('gx', 'gz'), scatter_dimension=0, tiled=True)  189 us
    all_to_all x1, blocking collectives, body(): lax.all_to_all(grad_block, 'gx', split_axis=1, concat_axis=0, tiled=True)  46.1 us
    all_gather x1, waiting for transfers between devices, body(): lax.all_gather(inputs_block, 'gx', axis=0, tiled=True)  43.9 us
    all_gather x1, waiting for transfers between devices, body(): grad_block = lax.all_gather(grad_out, 'gy', axis=1, tiled=True)  27.8 us
    all_gather x1, waiting for transfers between devices, body(): inputs_block = lax.all_gather(x_saved, 'gz', axis=1, tiled=True)  26.1 us
    dot_general x1, matrix products, body(): jnp.einsum('td,tc->dc', lax.all_gather(inputs_block, 'gx', axis=0, tiled=...  14.2 us
    dot_general x1, matrix products, body(): jnp.einsum('atc,bkc->abtk', grad_split, weight_split, preferred_element_t...  11.8 us
  transfers between devices with their start and end apart: 4, of which 4 were waited for; matrix products, arithmetic and copies ran while one was open for 10% of the time, Pallas kernels for 0%

commit v1 on v0

--- a/solution.py
+++ b/solution.py
@@ -1,7 +1,16 @@
+import functools
 import jax
 import jax.numpy as jnp
 from jax import lax
 from jax.sharding import PartitionSpec as P
+
+
+def vectors_assign(payload, comm_axis, array_dim):
+    block_now = jnp.stack(lax.axis_size(comm_axis) * [payload])
+    return jnp.concatenate(lax.all_to_all(block_now, comm_axis, 0, 0), axis=array_dim)
+
+
+_use_space = functools.partial(vectors_assign, comm_axis="gz", array_dim=1)
 
 
 def body(x_saved, grad_out, weight):
@@ -11,7 +20,7 @@
     grad_block = lax.all_gather(grad_out, "gy", axis=1, tiled=True)
     grad_all = lax.all_to_all(grad_block, "gx", split_axis=1, concat_axis=0, tiled=True)
     unit_cols = grad_all.shape[1]
-    inputs_block = lax.all_gather(x_saved, "gz", axis=1, tiled=True)
+    inputs_block = _use_space(x_saved)
     summed = jnp.einsum(
         "td,tc->dc",
         lax.all_gather(inputs_block, "gx", axis=0, tiled=True),

time: 387 us -> 372 us (0.961)
  waiting for transfers between devices: 288 us -> 258 us
  blocking collectives: 46.1 us -> 59 us
    all_gather x1 -> x0, waiting for transfers between devices: 26.1 us -> none  [body(): inputs_block = lax.all_gather(x_saved, 'gz', axis=1, tiled=True)]
    all_gather x1, waiting for transfers between devices: 27.8 us -> 7.88 us  [body(): grad_block = lax.all_gather(grad_out, 'gy', axis=1, tiled=True)]
    all_to_all x0 -> x1, blocking collectives: none -> 19.5 us  [vectors_assign(): lax.all_to_all(block_now, comm_axis, 0, 0)]
    all_gather x1, waiting for transfers between devices: 43.9 us -> 58.1 us  [body(): lax.all_gather(inputs_block, 'gx', axis=0, tiled=True)]
    all_to_all x1, blocking collectives: 46.1 us -> 39.5 us  [body(): lax.all_to_all(grad_block, 'gx', split_axis=1, concat_axis=0, tiled=True)]
  transfers between devices with their start and end apart: 4 -> 3, of which waited for: 4 -> 3; matrix products, arithmetic and copies ran while one was open for 10% -> 10% of each run, Pallas kernels for 0% -> 0%
where the time goes in v1:
time: 372 us; the launch traced here: 371 us
  waiting for transfers between devices  258 us (69%)
  blocking collectives  59 us (16%)
  matrix products  26 us (7%)
  between operations  13.8 us (4%)
  local copies, waits for them, and re-layouts  12.5 us (3%)
    reduce_scatter x1, waiting for transfers between devices, body(): lax.psum_scatter(terms, ('gx', 'gz'), scatter_dimension=0, tiled=True)  192 us
    all_gather x1, waiting for transfers between devices, body(): lax.all_gather(inputs_block, 'gx', axis=0, tiled=True)  58.1 us
    all_to_all x1, blocking collectives, body(): lax.all_to_all(grad_block, 'gx', split_axis=1, concat_axis=0, tiled=True)  39.5 us
    all_to_all x1, blocking collectives, vectors_assign(): lax.all_to_all(block_now, comm_axis, 0, 0)  19.5 us
    dot_general x1, matrix products, body(): jnp.einsum('td,tc->dc', lax.all_gather(inputs_block, 'gx', axis=0, tiled=...  14.1 us
    dot_general x1, matrix products, body(): jnp.einsum('atc,bkc->abtk', grad_split, weight_split, preferred_element_t...  11.9 us
    all_gather x1, waiting for transfers between devices, body(): grad_block = lax.all_gather(grad_out, 'gy', axis=1, tiled=True)  7.88 us
  transfers between devices with their start and end apart: 3, of which 3 were waited for; matrix products, arithmetic and copies ran while one was open for 10% of the time, Pallas kernels for 0%

profile of v1, /device:TPU:0, one launch (start us, length us, event | category | flops | bytes accessed | tf_op | source)
XLA Modules:
  0.0 371.2 jit_solution(13003278977156362469)
XLA Ops:
  7.2 0.0 all-gather.3.cloned.1.call-start
  7.2 2.0 copy.5
  9.2 0.0 all-gather.3.cloned.1.call-update
  9.2 0.0 all-gather.5.cloned.1.call-start
  9.3 1.1 copy.8
  10.4 0.1 stack.2
  10.5 19.5 %all_to_all.24 = bf16[4,128,1024]{1,2,0:T(8,128)(2,1)} all-to-all(bf16[4,128,1024]{1,2,0:T(8,128)(2,1)S(1)} %stack.2), channel_id=1, replica_groups=mesh['gx'=8,'gy'=4,'gz'=4] {'gz'}, dimensions={0} | all-to-all | bytes 2097152 | tf_op jit(solution)/shard_map/all_to_all | solution.py:10
  30.1 0.0 all-gather.5.cloned.1.call-update
  30.1 0.0 reduce-scatter.2.cloned.1.call-start
  30.2 7.9 %all-gather.3.cloned.1.call-done = bf16[128,7168]{0,1:T(8,128)(2,1)} async-done(((bf16[128,1792]{0,1:T(8,128)(2,1)}), bf16[128,7168]{0,1:T(8,128)(2,1)}) %all-gather.3.cloned.1.call-update) | async-done | bytes 1835024 | tf_op jit(solution)/shard_map/all_gather | solution.py:20
  38.1 3.1 copy.6
  41.1 39.5 %all_to_all.25 = bf16[128,8,896]{2,0,1:T(8,128)(2,1)S(1)} all-to-all(bf16[128,8,896]{2,0,1:T(8,128)(2,1)S(1)} %copy.6), channel_id=1, replica_groups=mesh['gx'=8,'gy'=4,'gz'=4] {'gx'}, dimensions={1} | all-to-all | bytes 3670016 | tf_op jit(solution)/shard_map/all_to_all | solution.py:21
  80.6 0.0 copy-start
  80.6 11.9 %convolution_bitcast_fusion = f32[8,4,128,1024]{3,2,0,1:T(8,128)S(1)} fusion(bf16[4,1024,896,1]{2,1,3,0:T(8,128)(2,1)} %bitcast.26, bf16[128,8,896]{2,0,1:T(8,128)(2,1)S(1)} %all_to_all.25), kind=kOutput, calls=%fused_computation | convolution fusion | flops 7516192768 | bytes 25952256 | tf_op jit(solution)/shard_map/atc,bkc->abtk/dot_general | solution.py:33
  92.5 0.0 copy-done
  92.5 6.2 %copy.7 = f32[8,4,128,1024]{3,2,1,0:T(8,128)} copy(f32[8,4,128,1024]{3,2,0,1:T(8,128)S(1)} %convolution_bitcast_fusion) | data formatting | bytes 33554432 | tf_op jit(solution)/shard_map/atc,bkc->abtk/transpose | solution.py:33
  98.7 0.0 copy-start.1
  98.7 0.0 reduce-scatter.2.cloned.1.call-update
  98.7 58.1 %all-gather.5.cloned.1.call-done = bf16[1024,4096]{0,1:T(8,128)(2,1)} async-done(((bf16[128,4096]{0,1:T(8,128)(2,1)}), bf16[1024,4096]{0,1:T(8,128)(2,1)}) %all-gather.5.cloned.1.call-update) | async-done | bytes 8388624 | tf_op jit(solution)/shard_map/all_gather | solution.py:26
  156.8 0.0 copy-done.1
  156.8 14.1 %convolution_convert_fusion = bf16[4096,896]{1,0:T(8,128)(2,1)} fusion(bf16[1024,4096]{0,1:T(8,128)(2,1)} %all-gather.5.cloned.1.call-done, bf16[1024,896]{1,0:T(8,128)(2,1)S(1)} %bitcast.25), kind=kOutput, calls=%fused_computation.1 | convolution fusion | flops 7519862784 | bytes 17563648 | tf_op jit(solution)/shard_map/td,tc->dc/dot_general | solution.py:24
  170.9 192.0 %reduce-scatter.2.cloned.1.call-done = f32[128,1024]{1,0:T(8,128)} async-done(((f32[4096,1024]{1,0:T(8,128)}), f32[128,1024]{1,0:T(8,128)}) %reduce-scatter.2.cloned.1.call-update) | async-done | bytes 524304 | tf_op jit(solution)/shard_map/reduce_scatter | solution.py:37
  362.9 1.8 convert_element_type.6
Async XLA Ops:
  7.2 30.9 %all-gather.3.cloned.1.call-start = ((), (), s32[]{:S(2)}) async-start(), calls=%async_computation.3 | async-start | bytes 2293760 | tf_op jit(solution)/shard_map/all_gather | solution.py:20
  9.2 147.5 %all-gather.5.cloned.1.call-start = ((), (), s32[]{:S(2)}) async-start(), calls=%async_computation.5 | async-start | bytes 9437184 | tf_op jit(solution)/shard_map/all_gather | solution.py:26
  30.1 332.8 %reduce-scatter.2.cloned.1.call-start = ((), (), s32[]{:S(2)}) async-start(), calls=%async_computation.4 | async-start | bytes 17301504 | tf_op jit(solution)/shard_map/reduce_scatter | solution.py:37
  80.6 11.9 %copy-start = (bf16[128,8,896]{2,0,1:T(8,128)(2,1)}, bf16[128,8,896]{2,0,1:T(8,128)(2,1)S(1)}, u32[]{:S(2)}) copy-start(bf16[128,8,896]{2,0,1:T(8,128)(2,1)S(1)} %all_to_all.25) | copy-start | bytes 5505028
  98.7 58.1 %copy-start.1 = (bf16[128,8,896]{2,0,1:T(8,128)(2,1)S(1)}, bf16[128,8,896]{2,0,1:T(8,128)(2,1)}, u32[]{:S(2)}) copy-start(bf16[128,8,896]{2,0,1:T(8,128)(2,1)} %copy-done) | copy-start | bytes 5505028
Sparse Core Ops, SparseCore 0:
  10.2 27.7 all-gather.2
  39.6 117.1 all-gather.4
  159.2 203.6 reduce-scatter.1
